TPU v7x, 32 devices: a whole 2x2x4 slice. The times are simulated.
32 devices in a mesh: dp: 8 (over z, x), tensor: 4 (over y, core).
Axes of the slice: x: 2, y: 2, z: 4, core: 2. Of those that a mesh axis runs over, the one named last changes fastest.
Arguments:
- tokens: bfloat16 [16384, 768], P(('dp', 'tensor')), may hold values from -6 to 6
- cotangent: bfloat16 [16384, 768], P(('dp', 'tensor')), may hold values from -6 to 6
- seq_lengths: int32 [8, 2], P('dp'), may hold values from 256 to 1792, as said below
- w_query: bfloat16 [768, 768], P('dp', 'tensor'), may hold values from -0.21875 to 0.21875
- w_keyvalue: bfloat16 [768, 128], P('dp'), may hold values from -0.21875 to 0.21875
- w_out: bfloat16 [768, 768], P('dp', 'tensor'), may hold values from -3.5 to 3.5
- w_up: bfloat16 [768, 3072], P('dp', 'tensor'), may hold values from -0.21875 to 0.21875
- w_down: bfloat16 [768, 3072], P('dp', 'tensor'), may hold values from -0.109375 to 0.109375
- norm1_gain: bfloat16 [768], P('dp'), may hold values from 0.5 to 1.5
- norm1_bias: bfloat16 [768], P('dp'), may hold values from -3 to 3
- norm2_gain: bfloat16 [768], P('dp'), may hold values from 0.5 to 1.5
- norm2_bias: bfloat16 [768], P('dp'), may hold values from -3 to 3
Outputs:
- out_tokens: bfloat16 [16384, 768], P(('dp', 'tensor'))
- d_tokens: float32 [16384, 768], P(('dp', 'tensor'))
- d_query: float32 [768, 768], P('dp', 'tensor')
- d_keyvalue: float32 [768, 128], P('dp')
- d_out_weight: float32 [768, 768], P('dp', 'tensor')
- d_up: float32 [768, 3072], P('dp', 'tensor')
- d_down: float32 [768, 3072], P('dp', 'tensor')
- d_norm1_gain: float32 [768], P('dp')
- d_norm1_bias: float32 [768], P('dp')
- d_norm2_gain: float32 [768], P('dp')
- d_norm2_bias: float32 [768], P('dp')
Inputs may be any that keep to these rules, and one draw needn't show every extreme that they name: `seq_lengths`: each row holds the length of its pack's one sequence, from 1024 to 1792, then the padding after it; a row sums to 2048, and in some row the sequence is exactly 1792 long.
All inputs are finite; a program needn't handle non-finite values.
Results may differ from a plain program's by a relative error of at most 0.011.
Values may be sent and summed in bfloat16 or wider, within the bound.
A program may use at most 256 MiB of HBM per device.

v0:
```python
import math

import jax
import jax.numpy as jnp
from jax import lax
from jax.sharding import PartitionSpec as P

ROT = 16
BLOCK = 512


EPS = 1e-05
NEG = -1e30


def slot_tables(seq_lengths, pack_rows):
    seq_sizes = seq_lengths.reshape(-1)
    seq_ends = jnp.cumsum(seq_sizes)
    slot_index = lax.iota(jnp.int32, pack_rows)
    passed = (slot_index[:, None] >= seq_ends[None, :]).astype(jnp.int32)
    segment = jnp.sum(passed, axis=1)
    position = slot_index - jnp.sum(passed * seq_sizes[None, :], axis=1)
    valid = (segment < seq_sizes.shape[0] - 1).astype(jnp.float32)
    return (segment, position, valid)


def rotary_tables(position, rot):
    half_rot = rot // 2
    exponent = lax.iota(jnp.int32, half_rot).astype(jnp.float32) * (-2.0 / rot)
    inv_freq = jnp.exp(exponent * math.log(10000.0))
    angles = position.astype(jnp.float32)[:, None] * inv_freq[None, :]
    return (jnp.cos(angles), jnp.sin(angles))


def rotate(field, cosine, sine, rot):
    half_rot = rot // 2
    first = field[..., :half_rot]
    second = field[..., half_rot:rot]
    cos_b = cosine[:, None, :]
    sin_b = sine[:, None, :]
    return jnp.concatenate(
        [first * cos_b - second * sin_b, second * cos_b + first * sin_b, field[..., rot:]], axis=-1
    )


def rotate_back(grad, cosine, sine, rot):
    half_rot = rot // 2
    first = grad[..., :half_rot]
    second = grad[..., half_rot:rot]
    cos_b = cosine[:, None, :]
    sin_b = sine[:, None, :]
    return jnp.concatenate(
        [first * cos_b + second * sin_b, second * cos_b - first * sin_b, grad[..., rot:]], axis=-1
    )


def norm_stats(token_f):
    mean = jnp.mean(token_f, axis=-1, keepdims=True)
    centered = token_f - mean
    inv_std = lax.rsqrt(jnp.mean(centered * centered, axis=-1, keepdims=True) + EPS)
    return (centered * inv_std, inv_std)


def norm_back(d_scaled, scaled, inv_std):
    return inv_std * (
        d_scaled
        - jnp.mean(d_scaled, axis=-1, keepdims=True)
        - scaled * jnp.mean(d_scaled * scaled, axis=-1, keepdims=True)
    )


def contract_rows(left, right):
    return lax.dot_general(
        left, right, (((0,), (0,)), ((), ())), preferred_element_type=jnp.float32
    )


def contract_cols(left, right):
    return lax.dot_general(
        left, right, (((1,), (1,)), ((), ())), preferred_element_type=jnp.float32
    )


def visible(segment, first, block_rows, key_len):
    row_index = first + lax.iota(jnp.int32, block_rows)
    key_index = lax.iota(jnp.int32, key_len)
    same = segment[first : first + block_rows][:, None] == segment[:key_len][None, :]
    return same & (key_index[None, :] <= row_index[:, None])


def block_scores(q_block, keys, segment, first, block_rows, scale):
    key_len = first + block_rows
    scores = (
        jnp.einsum("qhd,kd->hqk", q_block, keys[:key_len], preferred_element_type=jnp.float32)
        * scale
    )
    return jnp.where(visible(segment, first, block_rows, key_len)[None], scores, NEG)


def attend_forward(queries, keys, values, segment, block_rows, scale):
    outputs = []
    totals = []
    for index in range(queries.shape[0] // block_rows):
        first = index * block_rows
        key_len = first + block_rows
        scores = block_scores(queries[first:key_len], keys, segment, first, block_rows, scale)
        top = jnp.max(scores, axis=-1, keepdims=True)
        expd = jnp.exp(scores - top)
        total = jnp.sum(expd, axis=-1, keepdims=True)
        probs = (expd / total).astype(jnp.bfloat16)
        outputs.append(
            jnp.einsum("hqk,kd->qhd", probs, values[:key_len], preferred_element_type=jnp.float32)
        )
        totals.append(top + jnp.log(total))
    return (jnp.concatenate(outputs, axis=0), totals)


def attend_backward(queries, keys, values, d_attended, segment, totals, block_rows, scale):
    pack_rows, heads_dev, head = queries.shape
    d_queries = []
    d_keys = jnp.zeros((pack_rows, head), jnp.float32)
    d_values = jnp.zeros((pack_rows, head), jnp.float32)
    for index in range(pack_rows // block_rows):
        first = index * block_rows
        key_len = first + block_rows
        q_block = queries[first:key_len]
        scores = block_scores(q_block, keys, segment, first, block_rows, scale)
        probs = jnp.exp(scores - totals[index])
        d_block = d_attended[first:key_len]
        d_probs = jnp.einsum(
            "qhd,kd->hqk", d_block, values[:key_len], preferred_element_type=jnp.float32
        )
        delta = jnp.sum(probs * d_probs, axis=-1, keepdims=True)
        d_scores = (probs * (d_probs - delta)).astype(jnp.bfloat16)
        d_values = d_values.at[:key_len].add(
            jnp.einsum(
                "hqk,qhd->kd",
                probs.astype(jnp.bfloat16),
                d_block,
                preferred_element_type=jnp.float32,
            )
        )
        d_queries.append(
            jnp.einsum("hqk,kd->qhd", d_scores, keys[:key_len], preferred_element_type=jnp.float32)
            * scale
        )
        d_keys = d_keys.at[:key_len].add(
            jnp.einsum("hqk,qhd->kd", d_scores, q_block, preferred_element_type=jnp.float32) * scale
        )
    return (jnp.concatenate(d_queries, axis=0), d_keys, d_values)


def shards(
    tokens,
    cotangent,
    seq_lengths,
    w_query,
    w_keyvalue,
    w_out,
    w_up,
    w_down,
    norm1_gain,
    norm1_bias,
    norm2_gain,
    norm2_bias,
):
    own_rows = tokens.shape[0]
    pack_rows = own_rows * lax.axis_size("tensor")
    row_start = lax.axis_index("tensor") * own_rows
    segment, position, valid = slot_tables(seq_lengths, pack_rows)
    own_valid = lax.dynamic_slice_in_dim(valid, row_start, own_rows)
    gathered = (
        lax.all_gather(w_query, "dp", axis=0, tiled=True),
        lax.all_gather(w_keyvalue, "dp", axis=0, tiled=True),
        lax.all_gather(w_out, "dp", axis=0, tiled=True),
        lax.all_gather(w_up, "dp", axis=0, tiled=True),
        lax.all_gather(w_down, "dp", axis=0, tiled=True),
        lax.all_gather(norm1_gain, "dp", axis=0, tiled=True),
        lax.all_gather(norm1_bias, "dp", axis=0, tiled=True),
        lax.all_gather(norm2_gain, "dp", axis=0, tiled=True),
        lax.all_gather(norm2_bias, "dp", axis=0, tiled=True),
    )
    wq_all, wkv_all, wo_all, wup_all, wdown_all = gathered[:5]
    gain1 = gathered[5].astype(jnp.float32)
    bias1 = gathered[6].astype(jnp.float32)
    gain2 = gathered[7].astype(jnp.float32)
    bias2 = gathered[8].astype(jnp.float32)
    token_f = tokens.astype(jnp.float32)
    all_tokens, all_cot = (
        lax.all_gather(tokens, "tensor", axis=0, tiled=True),
        lax.all_gather(cotangent, "tensor", axis=0, tiled=True),
    )
    scaled_all, inv_all = norm_stats(all_tokens.astype(jnp.float32))
    scaled_own = lax.dynamic_slice_in_dim(scaled_all, row_start, own_rows)
    inv_own = lax.dynamic_slice_in_dim(inv_all, row_start, own_rows)
    normed1 = (scaled_all * gain1 + bias1).astype(jnp.bfloat16)
    normed2 = (scaled_all * gain2 + bias2).astype(jnp.bfloat16)
    head = wkv_all.shape[1] // 2
    heads_dev = wq_all.shape[1] // head
    scale = head ** (-0.5)
    cosine, sine = rotary_tables(position, ROT)
    query_pre = jnp.dot(normed1, wq_all, preferred_element_type=jnp.float32)
    kv_pre = jnp.dot(normed1, wkv_all, preferred_element_type=jnp.float32)
    queries = rotate(query_pre.reshape(pack_rows, heads_dev, head), cosine, sine, ROT).astype(
        jnp.bfloat16
    )
    keys = rotate(kv_pre[:, None, :head], cosine, sine, ROT)[:, 0].astype(jnp.bfloat16)
    values = kv_pre[:, head:].astype(jnp.bfloat16)
    attended_f, totals = attend_forward(queries, keys, values, segment, BLOCK, scale)
    attended = attended_f.reshape(pack_rows, heads_dev * head).astype(jnp.bfloat16)
    up_pre = jnp.dot(normed2, wup_all, preferred_element_type=jnp.float32)
    hidden = jax.nn.gelu(up_pre, approximate=False).astype(jnp.bfloat16)
    partial_mixed = contract_cols(attended, wo_all) + contract_cols(hidden, wdown_all)
    mixed = lax.psum_scatter(partial_mixed, "tensor", scatter_dimension=0, tiled=True)
    out_tokens = (token_f + mixed).astype(jnp.bfloat16)
    grad_all = all_cot.astype(jnp.float32) * valid[:, None]
    grad_low = grad_all.astype(jnp.bfloat16)
    d_out_weight = contract_rows(grad_low, attended)
    d_down = contract_rows(grad_low, hidden)
    d_attended = jnp.dot(grad_low, wo_all, preferred_element_type=jnp.float32).astype(jnp.bfloat16)
    d_hidden = jnp.dot(grad_low, wdown_all, preferred_element_type=jnp.float32)
    slope = 0.5 * (1.0 + lax.erf(up_pre * (1.0 / math.sqrt(2.0)))) + up_pre * jnp.exp(
        -0.5 * up_pre * up_pre
    ) * (1.0 / math.sqrt(2.0 * math.pi))
    d_up_pre = (d_hidden * slope).astype(jnp.bfloat16)
    d_up = contract_rows(normed2, d_up_pre)
    d_queries, d_keys, d_values = attend_backward(
        queries,
        keys,
        values,
        d_attended.reshape(pack_rows, heads_dev, head),
        segment,
        totals,
        BLOCK,
        scale,
    )
    d_query_pre = (
        rotate_back(d_queries, cosine, sine, ROT)
        .reshape(pack_rows, heads_dev * head)
        .astype(jnp.bfloat16)
    )
    d_keys_pre = rotate_back(d_keys[:, None, :], cosine, sine, ROT)[:, 0]
    d_kv_pre = jnp.concatenate([d_keys_pre, d_values], axis=1).astype(jnp.bfloat16)
    d_query = contract_rows(normed1, d_query_pre)
    d_keyvalue = contract_rows(normed1, d_kv_pre)
    d_normed1 = contract_cols(d_query_pre, wq_all) + contract_cols(d_kv_pre, wkv_all)
    d_normed2 = contract_cols(d_up_pre, wup_all)
    own_grad = cotangent.astype(jnp.float32) * own_valid[:, None]
    own_d1, own_d2 = (
        lax.psum_scatter(d_normed1, "tensor", scatter_dimension=0, tiled=True),
        lax.psum_scatter(d_normed2, "tensor", scatter_dimension=0, tiled=True),
    )
    d_tokens = (
        own_grad
        + norm_back(own_d1 * gain1, scaled_own, inv_own)
        + norm_back(own_d2 * gain2, scaled_own, inv_own)
    )
    d_gain1 = jnp.sum(own_d1 * scaled_own, axis=0)
    d_bias1 = jnp.sum(own_d1, axis=0)
    d_gain2 = jnp.sum(own_d2 * scaled_own, axis=0)
    d_bias2 = jnp.sum(own_d2, axis=0)
    summed = (
        lax.psum_scatter(d_query, "dp", scatter_dimension=0, tiled=True),
        lax.psum_scatter(d_keyvalue, "dp", scatter_dimension=0, tiled=True),
        lax.psum_scatter(d_out_weight, "dp", scatter_dimension=0, tiled=True),
        lax.psum_scatter(d_up, "dp", scatter_dimension=0, tiled=True),
        lax.psum_scatter(d_down, "dp", scatter_dimension=0, tiled=True),
        lax.psum_scatter(d_gain1, "dp", scatter_dimension=0, tiled=True),
        lax.psum_scatter(d_bias1, "dp", scatter_dimension=0, tiled=True),
        lax.psum_scatter(d_gain2, "dp", scatter_dimension=0, tiled=True),
        lax.psum_scatter(d_bias2, "dp", scatter_dimension=0, tiled=True),
    )
    shared = lax.psum((summed[1], summed[5], summed[6], summed[7], summed[8]), "tensor")
    return (
        out_tokens,
        d_tokens,
        summed[0],
        shared[0],
        summed[2],
        summed[3],
        summed[4],
        shared[1],
        shared[2],
        shared[3],
        shared[4],
    )


def solution(mesh):
    return jax.shard_map(
        shards,
        mesh=mesh,
        in_specs=(
            P(("dp", "tensor"), None),
            P(("dp", "tensor"), None),
            P("dp", None),
            P("dp", "tensor"),
            P("dp", None),
            P("dp", "tensor"),
            P("dp", "tensor"),
            P("dp", "tensor"),
            P("dp"),
            P("dp"),
            P("dp"),
            P("dp"),
        ),
        out_specs=(
            P(("dp", "tensor"), None),
            P(("dp", "tensor"), None),
            P("dp", "tensor"),
            P("dp", None),
            P("dp", "tensor"),
            P("dp", "tensor"),
            P("dp", "tensor"),
            P("dp"),
            P("dp"),
            P("dp"),
            P("dp"),
        ),
        check_vma=False,
    )
```

profile of v0, /device:TPU:0, one launch (start us, length us, event | category | flops | bytes accessed | tf_op | source)
XLA Modules:
  0.0 775.4 jit_solution(15429687078983671304)
XLA Ops:
  17.6 23.3 %all-reduce.12 = (bf16[768]{0:T(1024)(128)(2,1)S(1)}, bf16[768]{0:T(1024)(128)(2,1)S(1)}, bf16[768]{0:T(1024)(128)(2,1)S(1)}, bf16[768]{0:T(1024)(128)(2,1)S(1)}) all-reduce(bf16[768]{0:T(1024)(128)(2,1)S(1)} %dynamic-update-slice.25, bf16[768]{0:T(1024)(128)(2,1)S(1)} %dynamic-update-slice.24, ...), channel_id=1, replica_groups=mesh['dp'=8,'tensor'=4] {'dp'}, use_global_device_ids=true, to_apply=%add.5 | all-reduce | flops 3072 | bytes 12288
  43.3 32.8 %all_gather.36 = bf16[768,128]{1,0:T(8,128)(2,1)} all-gather(bf16[96,128]{1,0:T(8,128)(2,1)} %param.36), channel_id=1, replica_groups=mesh['dp'=8,'tensor'=4] {'dp'}, dimensions={0}, use_global_device_ids=true | all-gather | bytes 221184 | tf_op jit(solution)/shard_map/all_gather | solution.py:174
  77.1 32.2 %all_gather.37 = bf16[768,192]{1,0:T(8,128)(2,1)S(1)} all-gather(bf16[96,192]{1,0:T(8,128)(2,1)} %param.35), channel_id=1, replica_groups=mesh['dp'=8,'tensor'=4] {'dp'}, dimensions={0}, use_global_device_ids=true | all-gather | bytes 331776 | tf_op jit(solution)/shard_map/all_gather | solution.py:173
  109.2 33.8 %all_gather.38 = bf16[768,192]{1,0:T(8,128)(2,1)} all-gather(bf16[96,192]{1,0:T(8,128)(2,1)} %param.37), channel_id=1, replica_groups=mesh['dp'=8,'tensor'=4] {'dp'}, dimensions={0}, use_global_device_ids=true | all-gather | bytes 331776 | tf_op jit(solution)/shard_map/all_gather | solution.py:175
  169.2 19.6 %fusion.15 = (bf16[2048,768]{1,0:T(8,128)(2,1)}, f32[2048,768]{1,0:T(8,128)}) fusion(bf16[768,768]{1,0:T(8,128)(2,1)} %all-gather.7.cloned.1.call-done, f32[768]{0:T(1024)S(1)} %copy-done.76, f32[768]{0:T(1024)S(1)} %copy-done.54, f32[2048]{0:T(1024)S(1)} %copy-done.52, f32[2048]{0:T(1024)S(1)} %broadcast_multiply_fusion, ...), kind=kOutput, calls=%fused_computation.31 | convolution fusion | flops 2527592448 | bytes 13785088 | tf_op jit(solution)/shard_map/dot_general | solution.py:211
  194.6 4.1 fusion.156
  198.7 5.4 fusion.155
  204.1 7.4 fusion.21
  213.3 5.0 fusion.161
  222.2 9.3 %fusion.36 = f32[3,512]{1,0:T(4,128)} fusion(f32[3,512,1024]{1,2,0:T(8,128)} %get-tuple-element.179, f32[3,512]{1,0:T(4,128)S(1)} %get-tuple-element.178), kind=kLoop, calls=%fused_computation.68 | loop fusion | flops 3144192 | bytes 6303744 | tf_op jit(solution)/shard_map/reduce_sum | solution.py:109
  231.5 5.7 fusion.8
  241.0 5.4 fusion.24
  246.4 4.8 fusion.26
  253.6 6.4 fusion.5
  260.0 11.2 %fusion.7 = bf16[3,512,1536]{1,2,0:T(8,128)(2,1)} fusion(f32[1536,512,3]{1,0,2:T(8,128)} %get-tuple-element.185, f32[3,512,1536]{1,2,0:T(8,128)} %get-tuple-element.177, f32[3,512]{1,0:T(4,128)} %get-tuple-element.184, f32[3,512]{1,0:T(4,128)S(1)} %log_add_fusion.1), kind=kLoop, calls=%fused_computation.17 | loop fusion | flops 9437184 | bytes 23605248 | tf_op jit(solution)/shard_map/convert_element_type | solution.py:134
  271.2 4.0 fusion.64
  275.2 6.1 fusion
  283.5 5.2 fusion.2
  288.6 4.9 fusion.58
  328.9 5.1 fusion.159
  339.4 4.8 fusion.147
  344.3 4.0 fusion.162
  348.6 6.5 fusion.111
  355.2 7.1 fusion.146
  369.6 37.1 %all-reduce.10 = (f32[768]{0:T(1024)S(1)}, f32[768]{0:T(1024)S(1)}, f32[768]{0:T(1024)S(1)}, f32[768]{0:T(1024)S(1)}) all-reduce(f32[768]{0:T(1024)S(1)} %get-tuple-element.128, f32[768]{0:T(1024)S(1)} %get-tuple-element.131, f32[768]{0:T(1024)S(1)} %get-tuple-element.123, ...), channel_id=10, replica_groups=mesh['dp'=8,'tensor'=4] {'dp'}, use_global_device_ids=true, to_apply=%region_31.32.clone | all-reduce | flops 3072 | bytes 24576
  407.0 23.9 %reduce-scatter.17.cloned.1.call-done = f32[96,128]{1,0:T(8,128)} async-done(((f32[768,128]{1,0:T(8,128)}), f32[96,128]{1,0:T(8,128)}) %reduce-scatter.17.cloned.1.call-update) | async-done | bytes 49168 | tf_op jit(solution)/shard_map/reduce_scatter | solution.py:264
  430.9 11.7 %all-reduce.11 = (f32[96,128]{1,0:T(8,128)}, f32[96]{0:T(128)}, f32[96]{0:T(128)}, f32[96]{0:T(128)}, f32[96]{0:T(128)}) all-reduce(f32[96,128]{1,0:T(8,128)} %reduce-scatter.17.cloned.1.call-done, f32[96]{0:T(128)S(1)} %dynamic-slice.65, f32[96]{0:T(128)S(1)} %dynamic-slice.67, ...), channel_id=1, replica_groups=mesh['dp'=8,'tensor'=4] {'tensor'}, use_global_device_ids=true, to_apply=%region_26.27 | all-reduce | flops 12672 | bytes 101376 | tf_op jit(solution)/shard_map/psum | solution.py:273
  442.6 48.2 %reduce-scatter.9.cloned.1.call-done = f32[512,768]{1,0:T(8,128)} async-done(((f32[2048,768]{1,0:T(8,128)}), f32[512,768]{1,0:T(8,128)}) %reduce-scatter.9.cloned.1.call-update) | async-done | bytes 1572880 | tf_op jit(solution)/shard_map/reduce_scatter | solution.py:214
  496.6 61.0 %reduce-scatter.19.cloned.1.call-done = f32[96,192]{1,0:T(8,128)} async-done(((f32[768,192]{1,0:T(8,128)}), f32[96,192]{1,0:T(8,128)}) %reduce-scatter.19.cloned.1.call-update) | async-done | bytes 73744 | tf_op jit(solution)/shard_map/reduce_scatter | solution.py:265
  557.6 65.2 %reduce-scatter.15.cloned.1.call-done = f32[96,192]{1,0:T(8,128)} async-done(((f32[768,192]{1,0:T(8,128)}), f32[96,192]{1,0:T(8,128)}) %reduce-scatter.15.cloned.1.call-update) | async-done | bytes 73744 | tf_op jit(solution)/shard_map/reduce_scatter | solution.py:263
  622.8 72.8 %reduce-scatter.21.cloned.1.call-done = f32[96,768]{1,0:T(8,128)} async-done(((f32[768,768]{1,0:T(8,128)}), f32[96,768]{1,0:T(8,128)}) %reduce-scatter.21.cloned.1.call-update) | async-done | bytes 294928 | tf_op jit(solution)/shard_map/reduce_scatter | solution.py:266
  695.5 72.6 %reduce-scatter.23.cloned.1.call-done = f32[96,768]{1,0:T(8,128)} async-done(((f32[768,768]{1,0:T(8,128)}), f32[96,768]{1,0:T(8,128)}) %reduce-scatter.23.cloned.1.call-update) | async-done | bytes 294928 | tf_op jit(solution)/shard_map/reduce_scatter | solution.py:267
  (345 shorter events, 111.4 us)
Async XLA Ops:
  7.2 141.5 %all-gather.5.cloned.1.call-start = ((), (), s32[]{:S(2)}) async-start(), calls=%async_computation.8 | async-start | bytes 3932160 | tf_op jit(solution)/shard_map/all_gather | solution.py:190
  7.9 153.4 %all-gather.11.cloned.1.call-start = ((), (), s32[]{:S(2)}) async-start(), calls=%async_computation.12 | async-start | bytes 3932160 | tf_op jit(solution)/shard_map/all_gather | solution.py:191
  8.7 160.5 %all-gather.7.cloned.1.call-start = ((), (), s32[]{:S(2)}) async-start(), calls=%async_computation.9 | async-start | bytes 1327104 | tf_op jit(solution)/shard_map/all_gather | solution.py:176
  9.4 194.7 %all-gather.9.cloned.1.call-start = ((), (), s32[]{:S(2)}) async-start(), calls=%async_computation.10 | async-start | bytes 1327104 | tf_op jit(solution)/shard_map/all_gather | solution.py:177
  10.0 353.2 %reduce-scatter.13.cloned.1.call-start = ((), (), s32[]{:S(2)}) async-start(), calls=%async_computation.14 | async-start | bytes 7864320 | tf_op jit(solution)/shard_map/reduce_scatter | solution.py:251
  10.0 144.1 %copy-start.73 = (f32[8]{0:T(128)}, f32[8]{0:T(128)S(1)}, u32[]{:S(2)}) copy-start(f32[8]{0:T(128)S(1)} %multiply_exponential_fusion) | copy-start | bytes 100
  43.3 116.3 %copy-start.45 = (f32[2048]{0:T(1024)}, f32[2048]{0:T(1024)S(1)}, u32[]{:S(2)}) copy-start(f32[2048]{0:T(1024)S(1)} %subtract_convert_fusion.2) | copy-start | bytes 24580
  109.2 56.3 %copy-start.13 = (bf16[768,192]{1,0:T(8,128)(2,1)}, bf16[768,192]{1,0:T(8,128)(2,1)S(1)}, u32[]{:S(2)}) copy-start(bf16[768,192]{1,0:T(8,128)(2,1)S(1)} %all_gather.37) | copy-start | bytes 884740
  151.2 18.0 %copy-start.47 = (f32[2048]{0:T(1024)}, f32[2048]{0:T(1024)S(1)}, u32[]{:S(2)}) copy-start(f32[2048]{0:T(1024)S(1)} %broadcast_multiply_fusion) | copy-start | bytes 24580
  168.6 20.2 %copy-start.56 = (f32[3,512]{1,0:T(4,128)}, f32[3,512]{1,0:T(4,128)S(1)}, u32[]{:S(2)}) copy-start(f32[3,512]{1,0:T(4,128)S(1)} %get-tuple-element.180) | copy-start | bytes 18436
  168.6 23.3 %copy-start.1 = (f32[3,512,512]{1,2,0:T(8,128)}, f32[3,512,512]{1,2,0:T(8,128)S(1)}, u32[]{:S(2)}) copy-start(f32[3,512,512]{1,2,0:T(8,128)S(1)} %get-tuple-element.181) | copy-start | bytes 9437188
  169.1 19.7 %copy-start.58 = (f32[3,512]{1,0:T(4,128)}, f32[3,512]{1,0:T(4,128)S(1)}, u32[]{:S(2)}) copy-start(f32[3,512]{1,0:T(4,128)S(1)} %fusion.51) | copy-start | bytes 18436
  169.1 19.7 %copy-start.27 = (bf16[512,192]{0,1:T(8,128)(2,1)S(1)}, bf16[512,192]{0,1:T(8,128)(2,1)}, u32[]{:S(2)}) copy-start(bf16[512,192]{0,1:T(8,128)(2,1)} %get-tuple-element.154) | copy-start | bytes 589828
  198.7 40.8 %copy-start.60 = (f32[3,512]{1,0:T(4,128)}, f32[3,512]{1,0:T(4,128)S(1)}, u32[]{:S(2)}) copy-start(f32[3,512]{1,0:T(4,128)S(1)} %get-tuple-element.178) | copy-start | bytes 18436
  204.1 27.4 %copy-start.62 = (f32[3,512]{1,0:T(4,128)}, f32[3,512]{1,0:T(4,128)S(1)}, u32[]{:S(2)}) copy-start(f32[3,512]{1,0:T(4,128)S(1)} %get-tuple-element.176) | copy-start | bytes 18436
  218.3 147.9 %reduce-scatter.11.cloned.1.call-start = ((), (), s32[]{:S(2)}) async-start(), calls=%async_computation.13 | async-start | bytes 7864320 | tf_op jit(solution)/shard_map/reduce_scatter | solution.py:250
  222.2 15.1 %copy-start = (f32[3,512,2048]{1,2,0:T(8,128)}, f32[3,512,2048]{1,2,0:T(8,128)S(1)}, u32[]{:S(2)}) copy-start(f32[3,512,2048]{1,2,0:T(8,128)S(1)} %get-tuple-element.173) | copy-start | bytes 37748740
  222.2 15.0 %copy-start.64 = (f32[3,512]{1,0:T(4,128)}, f32[3,512]{1,0:T(4,128)S(1)}, u32[]{:S(2)}) copy-start(f32[3,512]{1,0:T(4,128)S(1)} %get-tuple-element.172) | copy-start | bytes 18436
  281.3 13.4 %slice-start.23 = ((s8[4718592]{0:T(1024)(128)(4,1)}), s8[4194304]{0:T(1024)(128)(4,1)S(1)}, s32[]{:S(2)}) async-start(s8[4718592]{0:T(1024)(128)(4,1)} %bitcast.236), calls=%async_computation.43 | async-start | bytes 8388608
  283.5 11.3 %slice-start.24 = ((s8[4718592]{0:T(1024)(128)(4,1)}), s8[524288]{0:T(1024)(128)(4,1)S(1)}, s32[]{:S(2)}) async-start(s8[4718592]{0:T(1024)(128)(4,1)} %bitcast.236), calls=%async_computation.44 | async-start | bytes 1048576
  310.4 120.5 %reduce-scatter.17.cloned.1.call-start = ((), (), s32[]{:S(2)}) async-start(), calls=%async_computation.16 | async-start | bytes 442368 | tf_op jit(solution)/shard_map/reduce_scatter | solution.py:264
  328.8 162.0 %reduce-scatter.9.cloned.1.call-start = ((), (), s32[]{:S(2)}) async-start(), calls=%async_computation.11 | async-start | bytes 7864320 | tf_op jit(solution)/shard_map/reduce_scatter | solution.py:214
  338.7 9.9 %copy-start.5 = (bf16[2048,768]{1,0:T(8,128)(2,1)S(1)}, bf16[2048,768]{1,0:T(8,128)(2,1)}, u32[]{:S(2)}) copy-start(bf16[2048,768]{1,0:T(8,128)(2,1)} %all-gather.5.cloned.1.call-done) | copy-start | bytes 9437188
  338.7 9.9 %copy-start.48 = (f32[2048]{0:T(1024)S(1)}, f32[2048]{0:T(1024)}, u32[]{:S(2)}) copy-start(f32[2048]{0:T(1024)} %copy-done.47) | copy-start | bytes 24580
  338.7 9.9 %copy-start.53 = (f32[2048]{0:T(1024)S(1)}, f32[2048]{0:T(1024)}, u32[]{:S(2)}) copy-start(f32[2048]{0:T(1024)} %copy-done.51) | copy-start | bytes 24580
  338.7 218.9 %reduce-scatter.19.cloned.1.call-start = ((), (), s32[]{:S(2)}) async-start(), calls=%async_computation.17 | async-start | bytes 884736 | tf_op jit(solution)/shard_map/reduce_scatter | solution.py:265
  344.2 278.5 %reduce-scatter.15.cloned.1.call-start = ((), (), s32[]{:S(2)}) async-start(), calls=%async_computation.15 | async-start | bytes 884736 | tf_op jit(solution)/shard_map/reduce_scatter | solution.py:263
  348.3 347.2 %reduce-scatter.21.cloned.1.call-start = ((), (), s32[]{:S(2)}) async-start(), calls=%async_computation.18 | async-start | bytes 2654208 | tf_op jit(solution)/shard_map/reduce_scatter | solution.py:266
  355.1 11.1 %copy-start.50 = (f32[768]{0:T(1024)S(1)}, f32[768]{0:T(1024)}, u32[]{:S(2)}) copy-start(f32[768]{0:T(1024)} %convert_element_type.124) | copy-start | bytes 9220
  355.1 412.9 %reduce-scatter.23.cloned.1.call-start = ((), (), s32[]{:S(2)}) async-start(), calls=%async_computation.19 | async-start | bytes 2654208 | tf_op jit(solution)/shard_map/reduce_scatter | solution.py:267
  363.2 130.3 %copy-start.10 = (f32[512,768]{1,0:T(8,128)S(1)}, f32[512,768]{1,0:T(8,128)}, u32[]{:S(2)}) copy-start(f32[512,768]{1,0:T(8,128)} %reduce-scatter.13.cloned.1.call-done) | copy-start | bytes 4718596
  366.2 127.3 %copy-start.11 = (f32[512,768]{1,0:T(8,128)S(1)}, f32[512,768]{1,0:T(8,128)}, u32[]{:S(2)}) copy-start(f32[512,768]{1,0:T(8,128)} %reduce-scatter.11.cloned.1.call-done) | copy-start | bytes 4718596
  (86 other events, 341.5 us)
Sparse Core Ops, SparseCore 0:
  9.6 31.2 all-gather.4
  42.4 28.5 all-gather.10
  73.2 43.3 all-gather.6
  118.6 40.4 all-gather.8
  218.4 55.5 reduce-scatter.12
  310.5 55.6 reduce-scatter.10
  369.5 61.3 reduce-scatter.16
  433.4 57.3 reduce-scatter.8
  495.1 62.4 reduce-scatter.18
  561.3 61.3 reduce-scatter.14
  627.2 68.2 reduce-scatter.20
  699.8 68.1 reduce-scatter.22
where the time goes:
time: 784 us; the launch traced here: 775 us
  waiting for transfers between devices  349 us (45%)
  blocking collectives  171 us (22%)
  matrix products  141 us (18%)
  other arithmetic  72.1 us (9%)
  local copies, waits for them, and re-layouts  24 us (3%)
  between operations  17.3 us (2%)
    reduce_scatter x1, waiting for transfers between devices, shards(): lax.psum_scatter(d_up, 'dp', scatter_dimension=0, tiled=True)  72.8 us
    reduce_scatter x1, waiting for transfers between devices, shards(): lax.psum_scatter(d_down, 'dp', scatter_dimension=0, tiled=True)  72.6 us
    reduce_scatter x1, waiting for transfers between devices, shards(): lax.psum_scatter(d_query, 'dp', scatter_dimension=0, tiled=True)  65.2 us
    reduce_scatter x1, waiting for transfers between devices, shards(): lax.psum_scatter(d_out_weight, 'dp', scatter_dimension=0, tiled=True)  61 us
    unnamed x2, blocking collectives  60.4 us
    reduce_scatter x1, waiting for transfers between devices, shards(): lax.psum_scatter(partial_mixed, 'tensor', scatter_dimension=0, tiled=True)  48.2 us
    all_gather x1, blocking collectives, shards(): lax.all_gather(w_out, 'dp', axis=0, tiled=True)  33.8 us
    all_gather x1, blocking collectives, shards(): lax.all_gather(w_keyvalue, 'dp', axis=0, tiled=True)  32.8 us
  transfers between devices with their start and end apart: 12, of which 7 were waited for; matrix products, arithmetic and copies ran while one was open for 27% of the time, Pallas kernels for 0%

commit v1 on v0

--- a/solution.py
+++ b/solution.py
@@ -1,8 +1,11 @@
+import functools
 import math
 
 import jax
 import jax.numpy as jnp
 from jax import lax
+from jax.experimental import pallas as pl
+from jax.experimental.pallas import tpu as pltpu
 from jax.sharding import PartitionSpec as P
 
 ROT = 16
@@ -150,6 +153,234 @@
     return (jnp.concatenate(d_queries, axis=0), d_keys, d_values)
 
 
+MESH = pl.DeviceIdType.MESH
+ANY = pl.BlockSpec(memory_space=pl.ANY)
+INVMEM = pl.BlockSpec(memory_space=pltpu.VMEM)
+
+
+class Axis:
+    def __init__(self, name, size):
+        self.name, self.size, self.half = name, size, size // 2
+        self.me = lax.axis_index(name)
+        self.row, self.par = self.me // 2, self.me % 2
+        self.pair = self.me + 1 - 2 * self.par
+
+    def line(self, step):
+        return lax.rem(self.row + step + self.half, self.half) * 2 + self.par
+
+    def pair_line(self, step):
+        return lax.rem(self.row + step + self.half, self.half) * 2 + 1 - self.par
+
+    def greet(self, barrier):
+        for step in range(1, self.size):
+            peer = lax.rem(self.me + step, self.size)
+            pl.semaphore_signal(barrier, inc=1, device_id={self.name: peer}, device_id_type=MESH)
+        return self.size - 1
+
+
+def remote(src, dst, send, recv, axis, peer):
+    return pltpu.make_async_remote_copy(
+        src_ref=src, dst_ref=dst, send_sem=send, recv_sem=recv, device_id={axis.name: peer}, device_id_type=MESH
+    )
+
+
+class Gather:
+    def __init__(self, axis, src, dst, send, recv):
+        self.axis, self.src, self.dst, self.send, self.recv = axis, src, dst, send, recv
+
+    def own(self, index):
+        peer = self.axis.pair if index == 0 else self.axis.line(index)
+        return remote(self.src, self.dst.at[self.axis.me], self.send.at[index], self.recv.at[index], self.axis, peer)
+
+    def forward(self, step):
+        slot, index = self.dst.at[self.axis.line(-step)], self.axis.half + step
+        return remote(slot, slot, self.send.at[index], self.recv.at[index], self.axis, self.axis.pair)
+
+    def start_line(self):
+        for step in range(1, self.axis.half):
+            self.own(step).start()
+
+    def start_pair(self):
+        self.own(0).start()
+
+    def pass_on(self):
+        for step in range(1, self.axis.half):
+            self.own(step).wait_recv()
+            self.forward(step).start()
+
+    def finish(self):
+        self.own(0).wait_recv()
+        for step in range(1, self.axis.half):
+            self.forward(step).wait_recv()
+        for step in range(self.axis.half):
+            self.own(step).wait_send()
+        for step in range(1, self.axis.half):
+            self.forward(step).wait_send()
+
+
+def gather_kernel(sizes, names, *refs):
+    count = len(names)
+    srcs, dsts = refs[:count], refs[count : 2 * count]
+    sends, recvs = refs[2 * count : 3 * count], refs[3 * count : 4 * count]
+    local = refs[4 * count]
+    axes = {name: Axis(name, size) for name, size in sizes.items()}
+    barrier = pltpu.get_barrier_semaphore()
+    pl.semaphore_wait(barrier, sum(axis.greet(barrier) for axis in axes.values()))
+    gathers = [Gather(axes[n], *four) for n, *four in zip(names, srcs, dsts, sends, recvs)]
+    for gather in gathers:
+        gather.start_line()
+        gather.start_pair()
+    copies = [
+        pltpu.make_async_copy(g.src, g.dst.at[g.axis.me], local.at[i]) for i, g in enumerate(gathers)
+    ]
+    for copy in copies:
+        copy.start()
+    for gather in gathers:
+        gather.pass_on()
+    for gather in gathers:
+        gather.finish()
+    for copy in copies:
+        copy.wait()
+
+
+def gather_all(arrays, names, sizes):
+    shapes = [jax.ShapeDtypeStruct((sizes[n],) + a.shape, a.dtype) for a, n in zip(arrays, names)]
+    sems = [pltpu.SemaphoreType.DMA((sizes[n],)) for n in names]
+    return pl.pallas_call(
+        functools.partial(gather_kernel, sizes, names),
+        out_shape=shapes,
+        in_specs=[INVMEM] * len(arrays),
+        out_specs=[ANY] * len(arrays),
+        scratch_shapes=sems + sems + [pltpu.SemaphoreType.DMA((len(arrays),))],
+        compiler_params=pltpu.CompilerParams(collective_id=0, has_side_effects=True),
+        name="gather_inputs",
+    )(*arrays)
+
+
+class Reduce:
+    def __init__(self, axis, part, out, held, summed, last, send, recv):
+        self.axis, self.part, self.out = axis, part, out
+        self.held, self.summed, self.last, self.send, self.recv = held, summed, last, send, recv
+
+    def first(self, row):
+        block = self.part.at[2 * row + 1 - self.axis.par]
+        return remote(block, self.held.at[row], self.send.at[row], self.recv.at[row], self.axis, self.axis.pair)
+
+    def second(self, step):
+        row, index = lax.rem(self.axis.row + step, self.axis.half), self.axis.half + step
+        return remote(
+            self.summed.at[row], self.last.at[step - 1], self.send.at[index], self.recv.at[index],
+            self.axis, self.axis.line(step),
+        )
+
+    def start(self):
+        for row in range(self.axis.half):
+            self.first(row).start()
+
+    def add(self, row, target, own):
+        rows = self.part.shape[1]
+        chunk = 64 if rows % 64 == 0 and rows > 96 else rows
+
+        @pl.loop(0, rows // chunk)
+        def _(index):
+            at = pl.ds(index * chunk, chunk)
+            total = self.part[2 * row + self.axis.par, at].astype(jnp.float32) + self.held[row, at].astype(jnp.float32)
+            if own:
+                target[at] = total.astype(target.dtype)
+            else:
+                target[row, at] = total.astype(target.dtype)
+
+    def middle(self):
+        for row in range(self.axis.half):
+            self.first(row).wait()
+        for step in range(1, self.axis.half):
+            self.add(lax.rem(self.axis.row + step, self.axis.half), self.summed, False)
+            self.second(step).start()
+        self.add(self.axis.row, self.out, True)
+
+    def end(self):
+        rows = self.part.shape[1]
+        chunk = 64 if rows % 64 == 0 and rows > 96 else rows
+        for step in range(1, self.axis.half):
+            self.second(step).wait()
+
+        @pl.loop(0, rows // chunk)
+        def _(index):
+            at = pl.ds(index * chunk, chunk)
+            total = self.out[at]
+            for step in range(1, self.axis.half):
+                total = total + self.last[step - 1, at].astype(jnp.float32)
+            self.out[at] = total
+
+
+def reduce_kernel(sizes, names, shared, *refs):
+    count, n_shared = len(names), len(shared)
+    parts, refs = refs[:count], refs[count:]
+    outs, refs = refs[:count], refs[count:]
+    held, refs = refs[:count], refs[count:]
+    summed, refs = refs[:count], refs[count:]
+    last, refs = refs[:count], refs[count:]
+    sends, refs = refs[:count], refs[count:]
+    recvs, refs = refs[:count], refs[count:]
+    slots, refs = refs[:n_shared], refs[n_shared:]
+    s_sends, refs = refs[:n_shared], refs[n_shared:]
+    s_recvs = refs[:n_shared]
+    axes = {name: Axis(name, size) for name, size in sizes.items()}
+    barrier = pltpu.get_barrier_semaphore()
+    pl.semaphore_wait(barrier, sum(axis.greet(barrier) for axis in axes.values()))
+    reduces = [
+        Reduce(axes[n], *seven) for n, *seven in zip(names, parts, outs, held, summed, last, sends, recvs)
+    ]
+    for item in reduces:
+        item.start()
+    for item in reduces:
+        item.middle()
+    for item in reduces:
+        item.end()
+    axis = axes["tensor"]
+    copies = []
+    for i, k in enumerate(shared):
+        slots[i][axis.me] = outs[k][...]
+        for step in range(1, axis.size):
+            peer = lax.rem(axis.me + step, axis.size)
+            copies.append(
+                remote(slots[i].at[axis.me], slots[i].at[axis.me], s_sends[i].at[step], s_recvs[i].at[step], axis, peer)
+            )
+            copies[-1].start()
+    for copy in copies:
+        copy.wait()
+    for i, k in enumerate(shared):
+        total = slots[i][0]
+        for t in range(1, axis.size):
+            total = total + slots[i][t]
+        outs[k][...] = total
+
+
+def reduce_all(arrays, names, shared, sizes):
+    halves = [sizes[n] // 2 for n in names]
+    tails = [a.shape[1:] for a in arrays]
+    sems = [pltpu.SemaphoreType.DMA((sizes[n],)) for n in names]
+    nt = sizes["tensor"]
+    s_sems = [pltpu.SemaphoreType.DMA((nt,)) for _ in shared]
+    return pl.pallas_call(
+        functools.partial(reduce_kernel, sizes, names, shared),
+        out_shape=[jax.ShapeDtypeStruct(tail, jnp.float32) for tail in tails],
+        in_specs=[INVMEM] * len(arrays),
+        out_specs=[INVMEM] * len(arrays),
+        scratch_shapes=[pltpu.VMEM((h,) + tail, a.dtype) for h, tail, a in zip(halves, tails, arrays)] * 2
+        + [pltpu.VMEM((h - 1,) + tail, a.dtype) for h, tail, a in zip(halves, tails, arrays)]
+        + sems
+        + sems
+        + [pltpu.VMEM((nt,) + tails[k], jnp.float32) for k in shared]
+        + s_sems
+        + s_sems,
+        compiler_params=pltpu.CompilerParams(
+            collective_id=1, has_side_effects=True, vmem_limit_bytes=60 << 20
+        ),
+        name="reduce_outputs",
+    )(*arrays)
+
+
 def shards(
     tokens,
     cotangent,
@@ -169,27 +400,18 @@
     row_start = lax.axis_index("tensor") * own_rows
     segment, position, valid = slot_tables(seq_lengths, pack_rows)
     own_valid = lax.dynamic_slice_in_dim(valid, row_start, own_rows)
-    gathered = (
-        lax.all_gather(w_query, "dp", axis=0, tiled=True),
-        lax.all_gather(w_keyvalue, "dp", axis=0, tiled=True),
-        lax.all_gather(w_out, "dp", axis=0, tiled=True),
-        lax.all_gather(w_up, "dp", axis=0, tiled=True),
-        lax.all_gather(w_down, "dp", axis=0, tiled=True),
-        lax.all_gather(norm1_gain, "dp", axis=0, tiled=True),
-        lax.all_gather(norm1_bias, "dp", axis=0, tiled=True),
-        lax.all_gather(norm2_gain, "dp", axis=0, tiled=True),
-        lax.all_gather(norm2_bias, "dp", axis=0, tiled=True),
-    )
-    wq_all, wkv_all, wo_all, wup_all, wdown_all = gathered[:5]
-    gain1 = gathered[5].astype(jnp.float32)
-    bias1 = gathered[6].astype(jnp.float32)
-    gain2 = gathered[7].astype(jnp.float32)
-    bias2 = gathered[8].astype(jnp.float32)
+    sizes = {"dp": lax.axis_size("dp"), "tensor": lax.axis_size("tensor")}
+    norms = jnp.stack([norm1_gain, norm1_bias, norm2_gain, norm2_bias], axis=1)
+    pad = jnp.zeros((norms.shape[0], 124), norms.dtype)
+    mixed_in = jnp.concatenate([w_keyvalue, norms, pad], axis=1)
+    names = ("tensor", "dp", "dp", "dp", "dp", "dp", "tensor")
+    gathered = gather_all((tokens, w_query, mixed_in, w_up, w_out, w_down, cotangent), names, sizes)
+    gathered = [g.reshape((-1,) + g.shape[2:]) for g in gathered]
+    all_tokens, wq_all, kvn_all, wup_all, wo_all, wdown_all, all_cot = gathered
+    wkv_all = kvn_all[:, : w_keyvalue.shape[1]]
+    vectors = kvn_all[:, w_keyvalue.shape[1] : w_keyvalue.shape[1] + 4].astype(jnp.float32)
+    gain1, bias1, gain2, bias2 = (vectors[:, i] for i in range(4))
     token_f = tokens.astype(jnp.float32)
-    all_tokens, all_cot = (
-        lax.all_gather(tokens, "tensor", axis=0, tiled=True),
-        lax.all_gather(cotangent, "tensor", axis=0, tiled=True),
-    )
     scaled_all, inv_all = norm_stats(all_tokens.astype(jnp.float32))
     scaled_own = lax.dynamic_slice_in_dim(scaled_all, row_start, own_rows)
     inv_own = lax.dynamic_slice_in_dim(inv_all, row_start, own_rows)
@@ -211,8 +433,6 @@
     up_pre = jnp.dot(normed2, wup_all, preferred_element_type=jnp.float32)
     hidden = jax.nn.gelu(up_pre, approximate=False).astype(jnp.bfloat16)
     partial_mixed = contract_cols(attended, wo_all) + contract_cols(hidden, wdown_all)
-    mixed = lax.psum_scatter(partial_mixed, "tensor", scatter_dimension=0, tiled=True)
-    out_tokens = (token_f + mixed).astype(jnp.bfloat16)
     grad_all = all_cot.astype(jnp.float32) * valid[:, None]
     grad_low = grad_all.astype(jnp.bfloat16)
     d_out_weight = contract_rows(grad_low, attended)
@@ -246,44 +466,25 @@
     d_normed1 = contract_cols(d_query_pre, wq_all) + contract_cols(d_kv_pre, wkv_all)
     d_normed2 = contract_cols(d_up_pre, wup_all)
     own_grad = cotangent.astype(jnp.float32) * own_valid[:, None]
-    own_d1, own_d2 = (
-        lax.psum_scatter(d_normed1, "tensor", scatter_dimension=0, tiled=True),
-        lax.psum_scatter(d_normed2, "tensor", scatter_dimension=0, tiled=True),
-    )
-    d_tokens = (
-        own_grad
-        + norm_back(own_d1 * gain1, scaled_own, inv_own)
-        + norm_back(own_d2 * gain2, scaled_own, inv_own)
-    )
-    d_gain1 = jnp.sum(own_d1 * scaled_own, axis=0)
-    d_bias1 = jnp.sum(own_d1, axis=0)
-    d_gain2 = jnp.sum(own_d2 * scaled_own, axis=0)
-    d_bias2 = jnp.sum(own_d2, axis=0)
-    summed = (
-        lax.psum_scatter(d_query, "dp", scatter_dimension=0, tiled=True),
-        lax.psum_scatter(d_keyvalue, "dp", scatter_dimension=0, tiled=True),
-        lax.psum_scatter(d_out_weight, "dp", scatter_dimension=0, tiled=True),
-        lax.psum_scatter(d_up, "dp", scatter_dimension=0, tiled=True),
-        lax.psum_scatter(d_down, "dp", scatter_dimension=0, tiled=True),
-        lax.psum_scatter(d_gain1, "dp", scatter_dimension=0, tiled=True),
-        lax.psum_scatter(d_bias1, "dp", scatter_dimension=0, tiled=True),
-        lax.psum_scatter(d_gain2, "dp", scatter_dimension=0, tiled=True),
-        lax.psum_scatter(d_bias2, "dp", scatter_dimension=0, tiled=True),
-    )
-    shared = lax.psum((summed[1], summed[5], summed[6], summed[7], summed[8]), "tensor")
-    return (
-        out_tokens,
-        d_tokens,
-        summed[0],
-        shared[0],
-        summed[2],
-        summed[3],
-        summed[4],
-        shared[1],
-        shared[2],
-        shared[3],
-        shared[4],
-    )
+    d_scaled = d_normed1 * gain1 + d_normed2 * gain2
+    d_norms = jnp.stack(
+        [
+            jnp.sum(d_normed1 * scaled_all, axis=0),
+            jnp.sum(d_normed1, axis=0),
+            jnp.sum(d_normed2 * scaled_all, axis=0),
+            jnp.sum(d_normed2, axis=0),
+        ]
+    )
+    nd, nt = sizes["dp"], sizes["tensor"]
+    parts = [partial_mixed, d_scaled, d_out_weight, d_up, d_down, d_query, d_keyvalue]
+    names = ("tensor", "tensor") + ("dp",) * 6
+    parts = [p.astype(jnp.bfloat16).reshape(sizes[n], -1, p.shape[-1]) for p, n in zip(parts, names)]
+    parts.append(jnp.swapaxes(d_norms.reshape(4, nd, -1), 0, 1))
+    sums = reduce_all(parts, names, (6, 7), sizes)
+    mixed, d_scaled_own = sums[:2]
+    out_tokens = (token_f + mixed).astype(jnp.bfloat16)
+    d_tokens = own_grad + norm_back(d_scaled_own, scaled_own, inv_own)
+    return (out_tokens, d_tokens, sums[5], sums[6], sums[2], sums[3], sums[4]) + tuple(sums[7][i] for i in range(4))
 
 
 def solution(mesh):

time: 784 us -> 327 us (0.42)
  waiting for transfers between devices: 349 us -> 0 us
  blocking collectives: 171 us -> 0 us
  Pallas kernels: 0 us -> 119 us
  matrix products: 141 us -> 113 us
  between operations: 17.3 us -> 2.23 us
    reduce_scatter x8 -> x0, waiting for transfers between devices: 347 us -> none  [the longest x1 72.8 us: shards(): lax.psum_scatter(d_up, 'dp', scatter_dimension=0, tiled=True)]
    pallas_call x0 -> x2, Pallas kernels: none -> 119 us  [the longest x1 62.7 us: reduce_all(): pl.pallas_call(functools.partial(reduce_kernel, sizes, names, shared), ou...]
    all_gather x3 -> x0, blocking collectives: 98.8 us -> none  [the longest x1 33.8 us: shards(): lax.all_gather(w_out, 'dp', axis=0, tiled=True)]
    unnamed x2 -> x0, blocking collectives: 60.4 us -> none
    dot_general x5, matrix products: 26.2 us -> 12.2 us  [contract_rows(): lax.dot_general(left, right, (((0,), (0,)), ((), ())), preferred_element_...]
    reduce_sum x4, other arithmetic: 17.8 us -> 4.35 us  [attend_forward(): total = jnp.sum(expd, axis=-1, keepdims=True)]
    psum x1 -> x0, blocking collectives: 11.7 us -> none  [shards(): lax.psum((summed[1], summed[5], summed[6], summed[7], summed[8]), 'tensor')]
    unnamed x225 -> x199, local copies, waits for them, and re-layouts: 21.1 us -> 10 us
  transfers between devices with their start and end apart: 12 -> 0, of which waited for: 7 -> 0; matrix products, arithmetic and copies ran while one was open for 27% -> 0% of each run, Pallas kernels for 0% -> 0%
where the time goes in v1:
time: 327 us; the launch traced here: 325 us
  Pallas kernels  119 us (36%)
  matrix products  113 us (35%)
  other arithmetic  64.7 us (20%)
  local copies, waits for them, and re-layouts  25.9 us (8%)
    pallas_call x1, Pallas kernels, reduce_all(): pl.pallas_call(functools.partial(reduce_kernel, sizes, names, shared), ou...  62.7 us
    pallas_call x1, Pallas kernels, gather_all(): pl.pallas_call(functools.partial(gather_kernel, sizes, names), out_shape=...  56.5 us
    convert_element_type x4, other arithmetic, attend_backward(): d_scores = (probs * (d_probs - delta)).astype(jnp.bfloat16)  29.4 us
    dot_general x5, matrix products, contract_cols(): lax.dot_general(left, right, (((1,), (1,)), ((), ())), preferred_element_...  23.3 us
    dot_general x1, matrix products, shards(): up_pre = jnp.dot(normed2, wup_all, preferred_element_type=jnp.float32)  16.6 us
    dot_general x4, matrix products, attend_backward(): jnp.einsum('qhd,kd->hqk', d_block, values[:key_len], preferred_element_ty...  13.2 us
    dot_general x5, matrix products, contract_rows(): lax.dot_general(left, right, (((0,), (0,)), ((), ())), preferred_element_...  12.2 us
    dot_general x4, matrix products, attend_backward(): jnp.einsum('hqk,qhd->kd', d_scores, q_block, preferred_element_type=jnp.f...  11.6 us

profile of v1, /device:TPU:0, one launch (start us, length us, event | category | flops | bytes accessed | tf_op | source)
XLA Modules:
  0.0 324.6 jit_solution(6864442837033906425)
XLA Ops:
  14.0 56.5 %gather_inputs.1 = (bf16[4,512,768]{2,1,0:T(8,128)(2,1)}, bf16[8,96,192]{2,1,0:T(8,128)(2,1)}, bf16[8,96,256]{2,1,0:T(8,128)(2,1)}, bf16[8,96,768]{2,1,0:T(8,128...) custom-call(bf16[512,768]{1,0:T(8,128)(2,1)} %refs_0_.1, ...), custom_call_target="tpu_custom_call" | custom-call | tf_op jit(solution)/shard_map/gather_inputs/pallas_call | solution.py:249
  70.5 2.5 convert_reduce_fusion
  74.8 1.9 copy.75
  76.7 4.3 %fusion.21 = bf16[2048,768]{1,0:T(8,128)(2,1)} fusion(f32[2048]{0:T(1024)S(1)} %compare_convert_fusion, bf16[4,512,768]{2,1,0:T(8,128)(2,1)} %get-tuple-element.144), kind=kLoop, calls=%fused_computation.35 | loop fusion | flops 4718592 | bytes 6299648 | tf_op jit(solution)/shard_map/convert_element_type | solution.py:437
  81.0 1.9 multiply_convert_fusion
  90.2 3.3 %add_convert_fusion.4 = (bf16[4,512,768]{2,1,0:T(8,128)(2,1)S(1)}, bf16[4,512,768]{2,1,0:T(8,128)(2,1)}) fusion(bf16[4,512,768]{2,1,0:T(8,128)(2,1)S(1)} %copy-done.2, f32[768]{0:T(1024)S(1)} %copy-done.81, f32[768]{0:T(1024)S(1)} %get-tuple-element.161, f32[4,512]{1,0:T(4,128)S(1)} %get-tuple-element.188, f32[4,512]{1,0:T(4,128)S(1)} %get-tuple-element.194, ...), kind=kLoop, calls=%fused_computation.68 | loop fusion | flops 14155776 | bytes 9465856 | tf_op jit(solution)/shard_map/convert_element_type | solution.py:418
  108.1 12.3 %fusion.24 = bf16[3,512,1024]{1,2,0:T(8,128)(2,1)S(1)} fusion(f32[1024,512,3]{1,0,2:T(8,128)S(1)} %get-tuple-element.216, f32[3,512,1024]{1,2,0:T(8,128)S(1)} %get-tuple-element.208, f32[3,512]{1,0:T(4,128)S(1)} %get-tuple-element.215, f32[3,512]{1,0:T(4,128)S(1)} %log_add_fusion.2), kind=kLoop, calls=%fused_computation.40 | loop fusion | flops 6291456 | bytes 15740928 | tf_op jit(solution)/shard_map/convert_element_type | solution.py:137
  123.0 16.6 %fusion.12 = (bf16[2048,768]{1,0:T(8,128)(2,1)S(1)}, f32[2048,768]{1,0:T(8,128)S(1)}) fusion(bf16[2048,768]{1,0:T(8,128)(2,1)S(1)} %bitcast.295, bf16[768,768]{1,0:T(8,128)(2,1)S(1)} %bitcast.339), kind=kOutput, calls=%fused_computation.26 | convolution fusion | flops 2518155264 | bytes 13762560 | tf_op jit(solution)/shard_map/dot_general | solution.py:433
  139.6 3.8 %convolution_convert_fusion.1 = bf16[768,768]{1,0:T(8,128)(2,1)} fusion(bf16[2048,768]{1,0:T(8,128)(2,1)S(1)} %copy-done.22, bf16[2048,768]{1,0:T(8,128)(2,1)S(1)} %get-tuple-element.199), kind=kOutput, calls=%fused_computation.123 | convolution fusion | flops 2416508928 | bytes 7471104 | tf_op jit(solution)/shard_map/dot_general | solution.py:76
  143.4 4.1 %fusion.18 = bf16[2048,768]{1,0:T(8,128)(2,1)S(1)} fusion(f32[2048,768]{1,0:T(8,128)S(1)} %get-tuple-element.200, bf16[2048,768]{1,0:T(8,128)(2,1)S(1)} %bitcast.288, bf16[768,768]{1,0:T(8,128)(2,1)S(1)} %bitcast.341), kind=kOutput, calls=%fused_computation.32 | convolution fusion | flops 2431647744 | bytes 13762560 | tf_op jit(solution)/shard_map/dot_general | solution.py:441
  147.6 4.5 %fusion.155 = f32[2048,768]{1,0:T(8,128)} fusion(bf16[2048,768]{1,0:T(8,128)(2,1)S(1)} %get-tuple-element.199, bf16[768,768]{1,0:T(8,128)(2,1)S(1)} %bitcast.342), kind=kOutput, calls=%fused_computation.254 | convolution fusion | flops 2415919104 | bytes 10616832 | tf_op jit(solution)/shard_map/dot_general | solution.py:82
  152.1 4.6 %fusion.157 = f32[2048,768]{1,0:T(8,128)} fusion(bf16[2048,768]{1,0:T(8,128)(2,1)S(1)} %fusion.18, bf16[768,768]{1,0:T(8,128)(2,1)S(1)} %bitcast.340), kind=kOutput, calls=%fused_computation.256 | convolution fusion | flops 2415919104 | bytes 10616832 | tf_op jit(solution)/shard_map/dot_general | solution.py:82
  156.7 2.8 fusion.151
  162.6 2.4 fusion.86
  165.0 5.1 %fusion.5 = (f32[3,512]{1,0:T(4,128)S(1)}, f32[1536,512,3]{1,0,2:T(8,128)}) fusion(f32[3,512,1536]{1,2,0:T(8,128)S(1)} %get-tuple-element.206, f32[3,512]{1,0:T(4,128)S(1)} %log_add_fusion.1, bf16[512,3,64]{0,2,1:T(8,128)(2,1)S(1)} %bitcast.299, bf16[2048,128]{0,1:T(8,128)(2,1)S(1)} %copy-done.27), kind=kOutput, calls=%fused_computation.15 | convolution fusion | flops 309066240 | bytes 19281920 | tf_op jit(solution)/shard_map/qhd,kd->hqk/dot_general | solution.py:133
  170.1 11.1 %fusion.7 = bf16[3,512,1536]{1,2,0:T(8,128)(2,1)} fusion(f32[1536,512,3]{1,0,2:T(8,128)} %get-tuple-element.214, f32[3,512,1536]{1,2,0:T(8,128)} %copy-done.1, f32[3,512]{1,0:T(4,128)S(1)} %get-tuple-element.213, f32[3,512]{1,0:T(4,128)S(1)} %log_add_fusion.1), kind=kLoop, calls=%fused_computation.17 | loop fusion | flops 9437184 | bytes 23605248 | tf_op jit(solution)/shard_map/convert_element_type | solution.py:137
  181.2 5.0 %fusion.63 = f32[2048,64]{0,1:T(8,128)} fusion(f32[2048,64]{0,1:T(8,128)} %copy-done.18, bf16[3,512,1536]{1,2,0:T(8,128)(2,1)} %fusion.7, bf16[2048,3,64]{0,2,1:T(8,128)(2,1)} %copy-done.21), kind=kOutput, calls=%fused_computation.109 | convolution fusion | flops 302186496 | bytes 5701632 | tf_op jit(solution)/shard_map/hqk,qhd->kd/dot_general | solution.py:151
  187.8 3.4 %fusion.149 = (f32[3,512]{1,0:T(4,128)S(1)}, f32[3,512,2048]{1,2,0:T(8,128)S(1)}) fusion(bf16[2048,3,64]{0,2,1:T(8,128)(2,1)} %copy-done.21, bf16[2048,1,48]{0,2,1:T(8,128)(2,1)S(1)} %slice.492, bf16[2048,1,8]{0,2,1:T(8,128)(2,1)S(1)} %copy-done.56, bf16[2048,1,8]{0,2,1:T(8,128)(2,1)S(1)} %copy-done.53, pred[512,2048]{0,1:T(8,128)(4,1)S(1)} %copy-done.43), kind=kOutput, calls=%fused_computation.248 | convolution fusion | flops 412875264 | bytes 14096384 | tf_op jit(solution)/shard_map/qhd,kd->hqk/dot_general | solution.py:97
  193.1 2.8 fusion.73
  197.2 2.6 fusion.88
  199.8 2.7 add_convert_fusion.2
  206.0 6.3 %fusion = (f32[3,512]{1,0:T(4,128)S(1)}, f32[2048,512,3]{1,0,2:T(8,128)S(1)}) fusion(f32[3,512,2048]{1,2,0:T(8,128)} %copy-done, f32[3,512]{1,0:T(4,128)S(1)} %log_add_fusion, bf16[512,3,64]{0,2,1:T(8,128)(2,1)S(1)} %bitcast.297, bf16[2048,128]{0,1:T(8,128)(2,1)} %copy-done.26), kind=kOutput, calls=%fused_computation.2 | convolution fusion | flops 412088832 | bytes 25636864 | tf_op jit(solution)/shard_map/qhd,kd->hqk/dot_general | solution.py:133
  214.3 5.2 %fusion.2 = bf16[3,512,2048]{1,2,0:T(8,128)(2,1)} fusion(f32[2048,512,3]{1,0,2:T(8,128)S(1)} %get-tuple-element.212, f32[3,512,2048]{1,2,0:T(8,128)S(1)} %bitcast.283, f32[3,512]{1,0:T(4,128)S(1)} %get-tuple-element.211, f32[3,512]{1,0:T(4,128)S(1)} %log_add_fusion), kind=kLoop, calls=%fused_computation.4 | loop fusion | flops 12582912 | bytes 31469568 | tf_op jit(solution)/shard_map/convert_element_type | solution.py:137
  219.5 4.9 %fusion.57 = f32[2048,1,64]{0,2,1:T(8,128)S(1)} fusion(f32[2048,64]{0,1:T(8,128)S(1)} %copy-done.19, bf16[3,512,2048]{1,2,0:T(8,128)(2,1)} %fusion.2, bf16[2048,3,64]{0,2,1:T(8,128)(2,1)} %copy-done.21), kind=kOutput, calls=%fused_computation.104 | convolution fusion | flops 402915328 | bytes 7536640 | tf_op jit(solution)/shard_map/hqk,qhd->kd/dot_general | solution.py:151
  230.9 2.0 copy.93
  232.9 2.4 fusion.156
  235.3 9.1 %multiply_reduce_fusion.1 = (f32[768]{0:T(1024)S(1)}, f32[768]{0:T(1024)S(1)}, f32[768]{0:T(1024)S(1)}, f32[768]{0:T(1024)S(1)}, bf16[2048,768]{1,0:T(8,128)(2,1...) fusion(bf16[4,512,768]{2,1,0:T(8,128)(2,1)S(1)} %copy-done.3, f32[2048]{0:T(1024)S(1)} %bitcast.329, ...), kind=kOutput, calls=%fused_computation.45 | convolution fusion | flops 430437376 | bytes 29073408 | tf_op jit(solution)/shard_map/dot_general | solution.py:82
  244.4 3.7 %convolution_convert_fusion.2 = bf16[768,768]{1,0:T(8,128)(2,1)} fusion(bf16[2048,768]{1,0:T(8,128)(2,1)S(1)} %get-tuple-element.168, bf16[2048,768]{1,0:T(8,128)(2,1)S(1)} %copy-done.89), kind=kOutput, calls=%fused_computation.124 | convolution fusion | flops 2416508928 | bytes 7471104 | tf_op jit(solution)/shard_map/dot_general | solution.py:76
  249.1 62.7 %reduce_outputs.1 = (f32[512,768]{1,0:T(8,128)}, f32[512,768]{1,0:T(8,128)}, f32[96,192]{1,0:T(8,128)}, f32[96,768]{1,0:T(8,128)}, f32[96,768]{1,0:T(8,128)}, /*...) custom-call(bf16[4,512,768]{2,1,0:T(8,128)(2,1)} %bitcast.290, bf16[4,512,768]{2,1,0:T(8,128)(2,1)} %bitcast.284, ...), custom_call_target="tpu_custom_call" | custom-call | tf_op jit(solution)/shard_map/reduce_outputs/pallas_call | solution.py:365
  311.9 2.6 add_convert_fusion.6
  315.8 2.2 fusion.146
  318.1 3.0 multiply_add_fusion
  (286 shorter events, 64.3 us)
Async XLA Ops:
  0.7 89.0 %copy-start.84 = (f32[8]{0:T(128)}, f32[8]{0:T(128)S(1)}, u32[]{:S(2)}) copy-start(f32[8]{0:T(128)S(1)} %multiply_exponential_fusion) | copy-start | bytes 100
  2.3 87.4 %copy-start.65 = (f32[2048]{0:T(1024)}, f32[2048]{0:T(1024)S(1)}, u32[]{:S(2)}) copy-start(f32[2048]{0:T(1024)S(1)} %subtract_convert_fusion.2) | copy-start | bytes 24580
  70.5 10.5 %copy-start.2 = (bf16[4,512,768]{2,1,0:T(8,128)(2,1)S(1)}, bf16[4,512,768]{2,1,0:T(8,128)(2,1)}, u32[]{:S(2)}) copy-start(bf16[4,512,768]{2,1,0:T(8,128)(2,1)} %get-tuple-element.138) | copy-start | bytes 9437188
  73.1 12.4 %copy-start.69 = (f32[1,4,4,128]{3,1,2,0:T(4,128)}, f32[1,4,4,128]{3,1,2,0:T(4,128)S(1)}, u32[]{:S(2)}) copy-start(f32[1,4,4,128]{3,1,2,0:T(4,128)S(1)} %copy.111) | copy-start | bytes 24580
  74.8 10.7 %copy-start.80 = (f32[768]{0:T(1024)}, f32[768]{0:T(1024)S(1)}, u32[]{:S(2)}) copy-start(f32[768]{0:T(1024)S(1)} %get-tuple-element.164) | copy-start | bytes 9220
  74.8 15.3 %copy-start.73 = (f32[768]{0:T(1024)}, f32[768]{0:T(1024)S(1)}, u32[]{:S(2)}) copy-start(f32[768]{0:T(1024)S(1)} %get-tuple-element.161) | copy-start | bytes 9220
  74.8 15.3 %copy-start.76 = (f32[768]{0:T(1024)}, f32[768]{0:T(1024)S(1)}, u32[]{:S(2)}) copy-start(f32[768]{0:T(1024)S(1)} %get-tuple-element.162) | copy-start | bytes 9220
  89.6 17.3 %copy-start.26 = (bf16[2048,128]{0,1:T(8,128)(2,1)}, bf16[2048,128]{0,1:T(8,128)(2,1)S(1)}, u32[]{:S(2)}) copy-start(bf16[2048,128]{0,1:T(8,128)(2,1)S(1)} %get-tuple-element.203) | copy-start | bytes 1572868
  90.1 97.7 %copy-start.31 = (bf16[2048,1,48]{0,2,1:T(8,128)(2,1)}, bf16[2048,1,48]{0,2,1:T(8,128)(2,1)S(1)}, u32[]{:S(2)}) copy-start(bf16[2048,1,48]{0,2,1:T(8,128)(2,1)S(1)} %slice.492) | copy-start | bytes 589828
  90.2 11.5 %copy-start.33 = (bf16[2048,1,64]{0,2,1:T(8,128)(2,1)}, bf16[2048,1,64]{0,2,1:T(8,128)(2,1)S(1)}, u32[]{:S(2)}) copy-start(bf16[2048,1,64]{0,2,1:T(8,128)(2,1)S(1)} %pad_maximum_fusion.7) | copy-start | bytes 786436
  95.1 25.3 %copy-start.21 = (bf16[2048,3,64]{0,2,1:T(8,128)(2,1)}, bf16[2048,3,64]{0,2,1:T(8,128)(2,1)S(1)}, u32[]{:S(2)}) copy-start(bf16[2048,3,64]{0,2,1:T(8,128)(2,1)S(1)} %pad_maximum_fusion.1) | copy-start | bytes 2359300
  123.0 16.6 %copy-start.22 = (bf16[2048,768]{1,0:T(8,128)(2,1)S(1)}, bf16[2048,768]{1,0:T(8,128)(2,1)}, u32[]{:S(2)}) copy-start(bf16[2048,768]{1,0:T(8,128)(2,1)} %fusion.21) | copy-start | bytes 9437188
  181.2 6.7 %copy-start.43 = (pred[512,2048]{0,1:T(8,128)(4,1)S(1)}, pred[512,2048]{0,1:T(8,128)(4,1)}, u32[]{:S(2)}) copy-start(pred[512,2048]{0,1:T(8,128)(4,1)} %fusion.41) | copy-start | bytes 3145732
  181.2 6.7 %copy-start.53 = (bf16[2048,1,8]{0,2,1:T(8,128)(2,1)S(1)}, bf16[2048,1,8]{0,2,1:T(8,128)(2,1)}, u32[]{:S(2)}) copy-start(bf16[2048,1,8]{0,2,1:T(8,128)(2,1)} %copy-done.52) | copy-start | bytes 98308
  181.2 6.7 %copy-start.56 = (bf16[2048,1,8]{0,2,1:T(8,128)(2,1)S(1)}, bf16[2048,1,8]{0,2,1:T(8,128)(2,1)}, u32[]{:S(2)}) copy-start(bf16[2048,1,8]{0,2,1:T(8,128)(2,1)} %copy-done.55) | copy-start | bytes 98308
  193.1 6.7 %slice-start.3 = ((s8[6291456]{0:T(1024)(128)(4,1)}), s8[4194304]{0:T(1024)(128)(4,1)S(1)}, s32[]{:S(2)}) async-start(s8[6291456]{0:T(1024)(128)(4,1)} %bitcast.293), calls=%async_computation.3 | async-start | bytes 8388608
  206.0 6.3 %slice-start = ((s8[12582912]{0:T(1024)(128)(4,1)}), s8[4194304]{0:T(1024)(128)(4,1)S(1)}, s32[]{:S(2)}) async-start(s8[12582912]{0:T(1024)(128)(4,1)} %bitcast.282), calls=%async_computation | async-start | bytes 8388608
  206.0 7.1 %slice-start.1 = ((s8[12582912]{0:T(1024)(128)(4,1)}), s8[4194304]{0:T(1024)(128)(4,1)S(1)}, s32[]{:S(2)}) async-start(s8[12582912]{0:T(1024)(128)(4,1)} %bitcast.282), calls=%async_computation.1 | async-start | bytes 8388608
  206.0 8.3 %slice-start.2 = ((s8[12582912]{0:T(1024)(128)(4,1)}), s8[4194304]{0:T(1024)(128)(4,1)S(1)}, s32[]{:S(2)}) async-start(s8[12582912]{0:T(1024)(128)(4,1)} %bitcast.282), calls=%async_computation.2 | async-start | bytes 8388608
  214.3 10.2 %copy-start.54 = (bf16[2048,1,8]{0,2,1:T(8,128)(2,1)S(1)}, bf16[2048,1,8]{0,2,1:T(8,128)(2,1)}, u32[]{:S(2)}) copy-start(bf16[2048,1,8]{0,2,1:T(8,128)(2,1)} %copy-done.52) | copy-start | bytes 98308
  214.3 10.2 %copy-start.57 = (bf16[2048,1,8]{0,2,1:T(8,128)(2,1)S(1)}, bf16[2048,1,8]{0,2,1:T(8,128)(2,1)}, u32[]{:S(2)}) copy-start(bf16[2048,1,8]{0,2,1:T(8,128)(2,1)} %copy-done.55) | copy-start | bytes 98308
  219.5 6.3 %copy-start.37 = (f32[512,3,64]{0,2,1:T(8,128)S(1)}, f32[512,3,64]{0,2,1:T(8,128)}, u32[]{:S(2)}) copy-start(f32[512,3,64]{0,2,1:T(8,128)} %fusion.82) | copy-start | bytes 1179652
  235.3 9.1 %copy-start.89 = (bf16[2048,768]{1,0:T(8,128)(2,1)S(1)}, bf16[2048,768]{1,0:T(8,128)(2,1)}, u32[]{:S(2)}) copy-start(bf16[2048,768]{1,0:T(8,128)(2,1)} %copy-done.88) | copy-start | bytes 9437188
  248.1 63.8 %copy-start.24 = (bf16[512,768]{1,0:T(8,128)(2,1)S(1)}, bf16[512,768]{1,0:T(8,128)(2,1)}, u32[]{:S(2)}) copy-start(bf16[512,768]{1,0:T(8,128)(2,1)} %refs_0_.1) | copy-start | bytes 2359300
  249.1 68.9 %copy-start.25 = (bf16[512,768]{1,0:T(8,128)(2,1)S(1)}, bf16[512,768]{1,0:T(8,128)(2,1)}, u32[]{:S(2)}) copy-start(bf16[512,768]{1,0:T(8,128)(2,1)} %refs_6_.1) | copy-start | bytes 2359300
  249.1 69.0 %copy-start.82 = (f32[512]{0:T(512)S(1)}, f32[512]{0:T(512)}, u32[]{:S(2)}) copy-start(f32[512]{0:T(512)} %dynamic_slice.9) | copy-start | bytes 6148
  249.1 69.0 %copy-start.83 = (f32[512,1]{0,1:T(1,128)S(1)}, f32[512,1]{0,1:T(1,128)}, u32[]{:S(2)}) copy-start(f32[512,1]{0,1:T(1,128)} %constant_dynamic-slice_fusion) | copy-start | bytes 6148
  311.8 9.2 %copy-start.68 = (f32[96,192]{1,0:T(8,128)S(1)}, f32[96,192]{1,0:T(8,128)}, u32[]{:S(2)}) copy-start(f32[96,192]{1,0:T(8,128)} %get-tuple-element.235) | copy-start | bytes 221188
  311.8 9.9 %copy-start.75 = (f32[96,128]{1,0:T(8,128)S(1)}, f32[96,128]{1,0:T(8,128)}, u32[]{:S(2)}) copy-start(f32[96,128]{1,0:T(8,128)} %get-tuple-element.236) | copy-start | bytes 147460
  311.9 10.5 %copy-start.67 = (f32[96,192]{1,0:T(8,128)S(1)}, f32[96,192]{1,0:T(8,128)}, u32[]{:S(2)}) copy-start(f32[96,192]{1,0:T(8,128)} %get-tuple-element.237) | copy-start | bytes 221188
  311.9 11.1 %copy-start.59 = (f32[96,768]{1,0:T(8,128)S(1)}, f32[96,768]{1,0:T(8,128)}, u32[]{:S(2)}) copy-start(f32[96,768]{1,0:T(8,128)} %get-tuple-element.238) | copy-start | bytes 884740
  311.9 11.8 %copy-start.58 = (f32[96,768]{1,0:T(8,128)S(1)}, f32[96,768]{1,0:T(8,128)}, u32[]{:S(2)}) copy-start(f32[96,768]{1,0:T(8,128)} %get-tuple-element.239) | copy-start | bytes 884740
  (63 other events, 210.5 us)
